TPU v7x, 32 devices: a whole 2x2x4 slice. The times are simulated.
32 devices in a mesh: ctx: 16 (over z, y, core), ch: 2 (over x).
Axes of the slice: x: 2, y: 2, z: 4, core: 2. Of those that a mesh axis runs over, the one named last changes fastest.
Arguments:
- projections: bfloat16 [3, 2048, 8192], P(None, 'ctx', 'ch'), may hold values from -150 to 150
- grouped_short_filters: float32 [3, 7, 512], P(None, None, 'ch'), may hold values from -2 to 2
- long_filter: float32 [2048, 8192], P('ctx', 'ch'), may hold values from 0 to 0.5
- norm_gain: float32 [8192], P('ch'), may hold values from 0.1 to 1.9
- out_grad: bfloat16 [2048, 8192], P('ctx', 'ch'), may hold values from -6 to 6
Outputs:
- output: bfloat16 [2048, 8192], P('ctx', 'ch')
- proj_grads: bfloat16 [3, 2048, 8192], P(None, 'ctx', 'ch')
- short_grads: float32 [3, 7, 512], P(None, None, 'ch')
- long_grad: float32 [2048, 8192], P('ctx', 'ch')
- gain_grad: float32 [8192], P('ch')
All inputs are finite; a program needn't handle non-finite values.
Results may differ from a plain program's by a relative error of at most 0.0064.
Values may be sent and summed in bfloat16 or wider, within the bound.
No kernel may reach another device: no remote copies, remote signals or barrier semaphores. Data moves between devices by JAX's collectives and lax.ppermute only.
A program may use at most 128 MiB of HBM per device.

v0:
```python
import math
import jax
import jax.numpy as jnp
from jax import lax
from jax.sharding import PartitionSpec as P

D = 8192
GROUP = 16
KS = 7
epsilon = 1e-05


def passed_along(block, axis, distance):
    devices = range(lax.axis_size(axis))
    route = [(i - distance, i) for i in devices if i - distance in devices]
    return lax.ppermute(block, axis, route)


def contract(form, left, right):
    return jnp.einsum(form, left, right, precision=lax.Precision.HIGHEST)


def factor_sizes(period):
    inner_len = 1
    while 2 * inner_len * (2 * inner_len) <= period and period % (4 * inner_len) == 0:
        inner_len = inner_len * 2
    return (period // inner_len, inner_len)


def dft_tables(order):
    ordinal_list = jnp.arange(order, dtype=jnp.int32)
    phases = (ordinal_list[:, None] * ordinal_list[None, :] % order).astype(jnp.float32) * (
        2.0 * math.pi / order
    )
    return (jnp.cos(phases), jnp.sin(phases))


def make_tables(outer_len, inner_len):
    period = outer_len * inner_len
    cos_a, sin_a = dft_tables(outer_len)
    cos_b, sin_b = dft_tables(inner_len)
    row_ids = jnp.arange(outer_len, dtype=jnp.int32)[:, None]
    col_ids = jnp.arange(inner_len, dtype=jnp.int32)[None, :]
    phases = (row_ids * col_ids % period).astype(jnp.float32) * (2.0 * math.pi / period)
    return (cos_a, sin_a, cos_b, sin_b, jnp.cos(phases), jnp.sin(phases))


def forward_spectrum(signal, tables):
    cos_a, sin_a, cos_b, sin_b, tw_cos, tw_sin = tables
    outer_len = cos_a.shape[0]
    inner_len = cos_b.shape[0]
    half_len = outer_len // 2
    channels = signal.shape[0]
    grid_rows = signal.reshape(channels, half_len, inner_len)
    real_a = contract("cnb,kn->ckb", grid_rows, cos_a[:, :half_len])
    imag_a = -contract("cnb,kn->ckb", grid_rows, sin_a[:, :half_len])
    real_t = real_a * tw_cos + imag_a * tw_sin
    imag_t = imag_a * tw_cos - real_a * tw_sin
    real_s = contract("ckb,bm->ckm", real_t, cos_b) + contract("ckb,bm->ckm", imag_t, sin_b)
    imag_s = contract("ckb,bm->ckm", imag_t, cos_b) - contract("ckb,bm->ckm", real_t, sin_b)
    return (real_s, imag_s)


def inverse_signal(real_s, imag_s, tables):
    cos_a, sin_a, cos_b, sin_b, tw_cos, tw_sin = tables
    outer_len = cos_a.shape[0]
    inner_len = cos_b.shape[0]
    half_len = outer_len // 2
    channels = real_s.shape[0]
    real_z = contract("ckb,bm->ckm", real_s, cos_b) - contract("ckb,bm->ckm", imag_s, sin_b)
    imag_z = contract("ckb,bm->ckm", imag_s, cos_b) + contract("ckb,bm->ckm", real_s, sin_b)
    real_t = real_z * tw_cos - imag_z * tw_sin
    imag_t = imag_z * tw_cos + real_z * tw_sin
    signal = contract("ckb,kn->cnb", real_t, cos_a[:, :half_len]) - contract(
        "ckb,kn->cnb", imag_t, sin_a[:, :half_len]
    )
    scale_back = 1.0 / (outer_len * inner_len)
    return (signal * scale_back).reshape(channels, half_len * inner_len)


def channel_sum(values):
    return lax.psum(values, "ch")


def on_device(projections, grouped_short_filters, long_filter, norm_gain, out_grad):
    tokens = projections.shape[1]
    spread = lax.axis_size("ctx")
    length = tokens * spread
    outer_len, inner_len = factor_sizes(2 * length)
    tables = make_tables(outer_len, inner_len)
    per_chan = jnp.repeat(grouped_short_filters, GROUP, axis=2)
    edge_rows = passed_along(projections[:, tokens - (KS - 1) :, :], "ctx", 1)
    extended = jnp.concatenate([edge_rows, projections], axis=1)
    conv_sum = jnp.zeros(projections.shape, jnp.float32)
    for tap_idx in range(KS):
        window = extended[:, KS - 1 - tap_idx : KS - 1 - tap_idx + tokens, :].astype(jnp.float32)
        conv_sum = conv_sum + per_chan[:, tap_idx, None, :] * window
    features = lax.optimization_barrier(conv_sum.astype(jnp.bfloat16))
    gate_feat = features[0].astype(jnp.float32)
    key_feat = features[1].astype(jnp.float32)
    value_feat = features[2].astype(jnp.float32)
    mixed_in = key_feat * value_feat
    chan_h = lax.all_to_all(long_filter.T, "ctx", split_axis=0, concat_axis=1, tiled=True)
    chan_u = lax.all_to_all(mixed_in.T, "ctx", split_axis=0, concat_axis=1, tiled=True)
    real_u, imag_u = forward_spectrum(chan_u, tables)
    real_h, imaginary_filter = forward_spectrum(chan_h, tables)
    prod_r = real_u * real_h - imag_u * imaginary_filter
    prod_i = real_u * imaginary_filter + imag_u * real_h
    chan_z = inverse_signal(prod_r, prod_i, tables)
    conv_out = lax.all_to_all(chan_z, "ctx", split_axis=1, concat_axis=0, tiled=True).T
    gated_out = gate_feat * conv_out
    sq_total = channel_sum(jnp.sum(gated_out * gated_out, axis=1))
    rscale = lax.rsqrt(sq_total / D + epsilon)
    normed = gated_out * rscale[:, None]
    output = (normed * norm_gain).astype(jnp.bfloat16)
    gradient_float = out_grad.astype(jnp.float32)
    scaled = gradient_float * norm_gain
    inner_total = channel_sum(jnp.sum(scaled * normed, axis=1))
    grad_gated = rscale[:, None] * (scaled - normed * (inner_total / D)[:, None])
    gain_part = jnp.sum(gradient_float * normed, axis=0)
    grad_conv = grad_gated * gate_feat
    grad_gate = grad_gated * conv_out
    cotangent_gate_input = lax.all_to_all(
        grad_conv.T, "ctx", split_axis=0, concat_axis=1, tiled=True
    )
    real_d, imag_d = forward_spectrum(cotangent_gate_input, tables)
    back_r = real_h * real_d + imaginary_filter * imag_d
    back_i = real_h * imag_d - imaginary_filter * real_d
    filt_r = real_u * real_d + imag_u * imag_d
    filt_i = real_u * imag_d - imag_u * real_d
    chan_du = inverse_signal(back_r, back_i, tables)
    chan_dh = inverse_signal(filt_r, filt_i, tables)
    mix_back = lax.all_to_all(chan_du, "ctx", split_axis=1, concat_axis=0, tiled=True)
    filt_back = lax.all_to_all(chan_dh, "ctx", split_axis=1, concat_axis=0, tiled=True)
    grad_mix = mix_back.T
    long_grad = filt_back.T
    grad_feats = jnp.stack([grad_gate, grad_mix * value_feat, grad_mix * key_feat])
    next_rows = passed_along(grad_feats[:, : KS - 1, :], "ctx", -1)
    cotangent_widened = jnp.concatenate([grad_feats, next_rows], axis=1)
    grad_in = jnp.zeros(grad_feats.shape, jnp.float32)
    tap_terms = []
    local_width = projections.shape[2]
    for tap_idx in range(KS):
        grad_in = (
            grad_in
            + per_chan[:, tap_idx, None, :] * cotangent_widened[:, tap_idx : tap_idx + tokens, :]
        )
        window = extended[:, KS - 1 - tap_idx : KS - 1 - tap_idx + tokens, :].astype(jnp.float32)
        tap_prod = jnp.sum(grad_feats * window, axis=1)
        tap_terms.append(jnp.sum(tap_prod.reshape(3, local_width // GROUP, GROUP), axis=2))
    filt_part = jnp.stack(tap_terms, axis=1)
    gain_grad, short_grads = lax.psum((gain_part, filt_part), "ctx")
    return (output, grad_in.astype(jnp.bfloat16), short_grads, long_grad, gain_grad)


def solution(mesh):
    in_specs = (P(None, "ctx", "ch"), P(None, None, "ch"), P("ctx", "ch"), P("ch"), P("ctx", "ch"))
    out_specs = (P("ctx", "ch"), P(None, "ctx", "ch"), P(None, None, "ch"), P("ctx", "ch"), P("ch"))
    return jax.shard_map(
        on_device, mesh=mesh, in_specs=in_specs, out_specs=out_specs, check_vma=False
    )
```

profile of v0, /device:TPU:0, one launch (start us, length us, event | category | flops | bytes accessed | tf_op | source)
XLA Modules:
  0.0 693.5 jit_solution(7625350813707377017)
XLA Ops:
  8.4 6.6 all-to-all-start.1
  27.5 26.1 %fusion.6 = bf16[3,128,4096]{1,2,0:T(8,128)(2,1)S(1)} fusion(bf16[3,128,4096]{1,2,0:T(8,128)(2,1)S(1)} %copy.105, f32[3,4096]{1,0:T(4,128)S(1)} %get-tuple-element.72, f32[3,4096]{1,0:T(4,128)S(1)} %get-tuple-element.73, f32[3,4096]{1,0:T(4,128)S(1)} %get-tuple-element.74, f32[3,4096]{1,0:T(4,128)S(1)} %get-tuple-element.75, ...), kind=kLoop, calls=%fused_computation.31 | loop fusion | flops 61341696 | bytes 6782976 | tf_op jit(solution)/shard_map/convert_element_type | solution.py:98
  56.8 11.0 %all-to-all-start = ((f32[16,256,128]{2,1,0:T(8,128)}), f32[16,256,128]{2,1,0:T(8,128)}, u32[]{:S(2)}, u32[]{:S(2)}) async-start(f32[16,256,128]{2,1,0:T(8,128)} %bitcast.237), calls=%async_computation | async-start | bytes 4194304 | tf_op jit(solution)/shard_map/all_to_all | solution.py:104
  70.3 5.8 fusion.91
  76.2 5.8 fusion.93
  82.0 26.8 %all-to-all-done = f32[16,256,128]{2,1,0:T(8,128)} async-done(((f32[16,256,128]{2,1,0:T(8,128)}), f32[16,256,128]{2,1,0:T(8,128)}, u32[]{:S(2)}, u32[]{:S(2)}) %all-to-all-start) | async-done | bytes 2097184 | tf_op jit(solution)/shard_map/all_to_all | solution.py:104
  110.7 5.8 fusion.95
  116.5 9.0 %add_bitcast_fusion.1 = (f32[256,64,64]{0,1,2:T(8,128)S(1)}, f32[256,64,64]{0,1,2:T(8,128)S(1)}, f32[256,64,64]{0,1,2:T(8,128)S(1)}, f32[256,64,64]{0,1,2:T(8,128)S(1)}) fusion(f32[64,256,64]{1,0,2:T(8,128)} %fusion.93, f32[64,256,64]{1,0,2:T(8,128)} %fusion.91, f32[64,64]{0,1:T(8,128)S(1)} %get-tuple-element.78, f32[64,64]{0,1:T(8,128)S(1)} %get-tuple-element.79, ...), kind=kOutput, calls=%fused_computation.80 | convolution fusion | flops 417333248 | bytes 31539200 | tf_op jit(solution)/shard_map/cnb,kn->ckb/dot_general | solution.py:20
  125.5 6.4 fusion.41
  132.0 6.9 fusion.43
  138.9 7.2 %fusion.49 = f32[256,64,64]{0,2,1:T(8,128)} fusion(f32[256,64,64]{0,1,2:T(8,128)S(1)} %get-tuple-element.69), kind=kOutput, calls=%fused_computation.99 | convolution fusion | flops 805363712 | bytes 8388608 | tf_op jit(solution)/shard_map/ckb,bm->ckm/dot_general | solution.py:20
  146.1 6.5 fusion.51
  152.6 7.3 %fusion.73 = f32[256,64,64]{0,2,1:T(8,128)S(1)} fusion(f32[256,64,64]{0,2,1:T(8,128)S(1)} %fusion.41, f32[256,64,64]{0,1,2:T(8,128)S(1)} %get-tuple-element.49), kind=kOutput, calls=%fused_computation.125 | convolution fusion | flops 806412288 | bytes 12582912 | tf_op jit(solution)/shard_map/ckb,bm->ckm/dot_general | solution.py:20
  159.8 7.3 %fusion.70 = f32[256,64,64]{0,2,1:T(8,128)} fusion(f32[256,64,64]{0,2,1:T(8,128)S(1)} %fusion.43, f32[256,64,64]{0,1,2:T(8,128)S(1)} %get-tuple-element.49), kind=kOutput, calls=%fused_computation.124 | convolution fusion | flops 806412288 | bytes 12582912 | tf_op jit(solution)/shard_map/ckb,bm->ckm/dot_general | solution.py:20
  167.1 7.2 %fusion.64 = f32[256,64,64]{0,2,1:T(8,128)} fusion(f32[256,64,64]{0,2,1:T(8,128)S(1)} %fusion.51, f32[256,64,64]{0,1,2:T(8,128)S(1)} %get-tuple-element.70), kind=kOutput, calls=%fused_computation.122 | convolution fusion | flops 806412288 | bytes 12582912 | tf_op jit(solution)/shard_map/ckb,bm->ckm/dot_general | solution.py:20
  174.3 11.9 %multiply_add_fusion.5 = (f32[256,64,64]{0,2,1:T(8,128)S(1)}, f32[256,64,64]{0,2,1:T(8,128)S(1)}, f32[256,64,64]{0,2,1:T(8,128)}) fusion(f32[256,64,64]{0,2,1:T(8,128)} %fusion.70, f32[256,64,64]{0,2,1:T(8,128)} %fusion.64, f32[256,64,64]{0,2,1:T(8,128)S(1)} %fusion.73, f32[256,64,64]{0,2,1:T(8,128)} %fusion.49, f32[256,64,64]{0,1,2:T(8,128)S(1)} %get-tuple-element.70), kind=kOutput, calls=%fused_computation.77 | convolution fusion | flops 812703744 | bytes 33554432 | tf_op jit(solution)/shard_map/ckb,bm->ckm/dot_general | solution.py:20
  195.0 4.8 convolution_subtract_fusion.2
  199.8 6.6 multiply_subtract_fusion.4
  210.9 4.9 multiply_bitcast_fusion.2
  218.3 11.3 %all-to-all-start.2 = ((f32[256,16,128]{0,2,1:T(8,128)}), f32[256,16,128]{0,2,1:T(8,128)}, u32[]{:S(2)}, u32[]{:S(2)}) async-start(f32[256,16,128]{0,2,1:T(8,128)} %bitcast.20), calls=%async_computation.2 | async-start | bytes 4194304 | tf_op jit(solution)/shard_map/all_to_all | solution.py:110
  232.0 38.6 %all-to-all-done.2 = f32[256,16,128]{0,2,1:T(8,128)} async-done(((f32[256,16,128]{0,2,1:T(8,128)}), f32[256,16,128]{0,2,1:T(8,128)}, u32[]{:S(2)}, u32[]{:S(2)}) %all-to-all-start.2) | async-done | bytes 2097184 | tf_op jit(solution)/shard_map/all_to_all | solution.py:110
  275.6 5.0 psum.28
  283.4 4.9 psum.29
  291.0 58.2 %all_to_all.105 = f32[16,256,128]{2,1,0:T(8,128)} all-to-all(f32[16,256,128]{2,1,0:T(8,128)S(1)} %bitcast.235), channel_id=1, replica_groups=mesh['ctx'=16,'ch'=2] {'ctx'}, dimensions={0} | all-to-all | bytes 4194304 | tf_op jit(solution)/shard_map/all_to_all | solution.py:123
  352.3 6.3 fusion.87
  358.6 6.0 add_bitcast_fusion
  364.6 6.9 fusion.33
  371.5 7.2 %fusion.35 = f32[256,64,64]{0,2,1:T(8,128)} fusion(f32[256,64,64]{0,1,2:T(8,128)S(1)} %get-tuple-element.46), kind=kOutput, calls=%fused_computation.85 | convolution fusion | flops 805363712 | bytes 8388608 | tf_op jit(solution)/shard_map/ckb,bm->ckm/dot_general | solution.py:20
  378.7 7.3 %fusion.79 = f32[256,64,64]{0,2,1:T(8,128)} fusion(f32[256,64,64]{0,2,1:T(8,128)S(1)} %fusion.33, f32[256,64,64]{0,1,2:T(8,128)S(1)} %get-tuple-element.45), kind=kOutput, calls=%fused_computation.127 | convolution fusion | flops 806412288 | bytes 12582912 | tf_op jit(solution)/shard_map/ckb,bm->ckm/dot_general | solution.py:20
  386.0 21.5 %multiply_subtract_fusion.1 = (f32[256,64,64]{0,2,1:T(8,128)}, f32[256,64,64]{0,2,1:T(8,128)}, f32[256,64,64]{0,2,1:T(8,128)}, f32[256,64,64]{0,2,1:T(8,128)}) fusion(f32[256,64,64]{0,2,1:T(8,128)} %get-tuple-element.71, f32[256,64,64]{0,2,1:T(8,128)} %fusion.64, f32[256,64,64]{0,2,1:T(8,128)} %fusion.79, f32[256,64,64]{0,2,1:T(8,128)} %copy-done.9, ...), kind=kOutput, calls=%fused_computation.67 | convolution fusion | flops 818995200 | bytes 46137344 | tf_op jit(solution)/shard_map/ckb,bm->ckm/dot_general | solution.py:20
  407.5 8.4 %fusion.121 = f32[256,64,64]{0,2,1:T(8,128)} fusion(f32[256,64,64]{0,2,1:T(8,128)} %get-tuple-element.31), kind=kOutput, calls=%fused_computation.188 | convolution fusion | flops 805363712 | bytes 8388608 | tf_op jit(solution)/shard_map/ckb,bm->ckm/dot_general | solution.py:20
  420.1 5.7 convolution_subtract_fusion
  434.3 5.6 convolution_subtract_fusion.1
  439.8 5.8 convolution_add_fusion.1
  445.6 11.7 %multiply_subtract_fusion = (f32[256,64,64]{0,2,1:T(8,128)}, f32[256,64,64]{0,2,1:T(8,128)}, f32[256,64,64]{0,2,1:T(8,128)}, f32[256,64,64]{0,2,1:T(8,128)S(1)}) fusion(f32[256,64,64]{0,2,1:T(8,128)} %convolution_subtract_fusion, f32[64,64]{1,0:T(8,128)S(1)} %copy.124, f32[64,64]{1,0:T(8,128)S(1)} %copy.123, f32[256,64,64]{0,2,1:T(8,128)} %convolution_subtract_fusion.1, ...), kind=kOutput, calls=%fused_computation.66 | convolution fusion | flops 818995200 | bytes 37781504 | tf_op jit(solution)/shard_map/ckb,bm->ckm/dot_general | solution.py:20
  457.3 7.4 %fusion.25 = f32[32,256,64]{1,0,2:T(8,128)S(1)} fusion(f32[256,64,64]{0,2,1:T(8,128)} %get-tuple-element.67, f32[64,64]{0,1:T(8,128)S(1)} %fusion.148), kind=kOutput, calls=%fused_computation.57 | convolution fusion | flops 402653184 | bytes 6307840 | tf_op jit(solution)/shard_map/ckb,kn->cnb/dot_general | solution.py:20
  464.7 4.7 multiply_bitcast_fusion.1
  471.9 5.4 all-to-all-start.4
  478.6 7.1 %fusion.21 = f32[32,256,64]{1,0,2:T(8,128)S(1)} fusion(f32[256,64,64]{0,2,1:T(8,128)} %get-tuple-element.42, f32[64,64]{0,1:T(8,128)S(1)} %fusion.148), kind=kOutput, calls=%fused_computation.53 | convolution fusion | flops 402653184 | bytes 6307840 | tf_op jit(solution)/shard_map/ckb,kn->cnb/dot_general | solution.py:20
  485.7 4.7 multiply_bitcast_fusion
  493.0 25.3 %all-to-all-done.4 = f32[256,16,128]{0,2,1:T(8,128)} async-done(((f32[256,16,128]{0,2,1:T(8,128)}), f32[256,16,128]{0,2,1:T(8,128)}, u32[]{:S(2)}, u32[]{:S(2)}) %all-to-all-start.4) | async-done | bytes 2097184 | tf_op jit(solution)/shard_map/all_to_all | solution.py:133
  518.3 11.5 %all-to-all-start.5 = ((f32[256,16,128]{0,2,1:T(8,128)}), f32[256,16,128]{0,2,1:T(8,128)}, u32[]{:S(2)}, u32[]{:S(2)}) async-start(f32[256,16,128]{0,2,1:T(8,128)} %bitcast.236), calls=%async_computation.5 | async-start | bytes 4194304 | tf_op jit(solution)/shard_map/all_to_all | solution.py:134
  538.0 21.9 %fusion.12 = (f32[3,4096]{1,0:T(4,128)S(1)}, f32[3,4096]{1,0:T(4,128)S(1)}, f32[3,4096]{1,0:T(4,128)S(1)}, f32[3,4096]{1,0:T(4,128)S(1)}, f32[3,4096]{1,0:T(4,12...) fusion(bf16[3,128,4096]{1,2,0:T(8,128)(2,1)S(1)} %copy-done.13, bf16[3,6,4096]{1,2,0:T(8,128)(2,1)S(1)} %copy-done.14, ...), kind=kLoop, calls=%fused_computation.37 | loop fusion | flops 64401408 | bytes 9928704 | tf_op jit(solution)/shard_map/reduce_sum | solution.py:149
  562.1 5.3 pad_maximum_fusion.1
  579.4 65.7 %all-reduce = (f32[3,7,256]{2,0,1:T(4,128)S(1)}, f32[4096]{0:T(1024)}) all-reduce(f32[3,7,256]{2,0,1:T(4,128)S(1)} %constant_dynamic-update-slice_fusion, f32[4096]{0:T(1024)S(1)} %get-tuple-element.27), channel_id=1, replica_groups=mesh['ctx'=16,'ch'=2] {'ctx'}, use_global_device_ids=true, to_apply=%region_18.19 | all-reduce | flops 9472 | bytes 75776 | tf_op jit(solution)/shard_map/psum | solution.py:152
  649.7 10.6 %pad_maximum_fusion = f32[3,134,4096]{1,2,0:T(8,128)} fusion(f32[3,6,4096]{1,2,0:T(8,128)} %copy.142, f32[1,128,4096]{1,2,0:T(8,128)} %copy-done.2, f32[1,128,4096]{1,2,0:T(8,128)} %copy-done, f32[1,128,4096]{1,2,0:T(8,128)S(1)} %bitcast.226), kind=kLoop, calls=%fused_computation | loop fusion | flops 4939776 | bytes 13172736 | tf_op jit(solution)/shard_map/concatenate | solution.py:139
  660.4 28.2 %fusion.15 = bf16[3,128,4096]{1,2,0:T(8,128)(2,1)} fusion(f32[3,134,4096]{1,2,0:T(8,128)} %pad_maximum_fusion, f32[3,4096]{1,0:T(4,128)S(1)} %copy-done.18, f32[3,4096]{1,0:T(4,128)S(1)} %copy-done.20, f32[3,4096]{1,0:T(4,128)S(1)} %copy-done.22, f32[3,4096]{1,0:T(4,128)S(1)} %copy-done.24, f32[3,4096]{1,0:T(4,128)S(1)} %copy-done.26, ...), kind=kLoop, calls=%fused_computation.41 | loop fusion | flops 25165824 | bytes 47529984 | tf_op jit(solution)/shard_map/convert_element_type | solution.py:153
  688.6 4.6 copy.148
  (135 shorter events, 105.5 us)
Async XLA Ops:
  2.3 12.7 %copy-start.31 = (f32[3,7,256]{2,1,0:T(8,128)S(1)}, f32[3,7,256]{2,1,0:T(8,128)}, u32[]{:S(2)}) copy-start(f32[3,7,256]{2,1,0:T(8,128)} %param.6) | copy-start | bytes 64516
  2.3 21.6 %collective-permute-start = (bf16[3,6,4096]{2,1,0:T(8,128)(2,1)}, bf16[3,6,4096]{2,1,0:T(8,128)(2,1)}, u32[]{:S(2)}, u32[]{:S(2)}) collective-permute-start(bf16[3,6,4096]{2,1,0:T(8,128)(2,1)} %slice.123), channel_id=1, source_target_pairs={{0,2},{2,4},{4,6},{6,8},{8,10},{10,12},{12,14},{14,16},{16,18},{18... | collective-permute-start | bytes 442376 | tf_op jit(solution)/shard_map/ppermute | solution.py:16
  8.4 48.4 %all-to-all-start.1 = ((f32[16,256,128]{2,1,0:T(8,128)}), f32[16,256,128]{2,1,0:T(8,128)}, u32[]{:S(2)}, u32[]{:S(2)}) async-start(f32[16,256,128]{2,1,0:T(8,128)} %bitcast.14), calls=%async_computation.1 | async-start | bytes 4194304 | tf_op jit(solution)/shard_map/all_to_all | solution.py:103
  18.4 9.1 %copy-start.17 = (f32[3,4096]{1,0:T(4,128)}, f32[3,4096]{1,0:T(4,128)S(1)}, u32[]{:S(2)}) copy-start(f32[3,4096]{1,0:T(4,128)S(1)} %get-tuple-element.72) | copy-start | bytes 147460
  18.4 9.1 %copy-start.19 = (f32[3,4096]{1,0:T(4,128)}, f32[3,4096]{1,0:T(4,128)S(1)}, u32[]{:S(2)}) copy-start(f32[3,4096]{1,0:T(4,128)S(1)} %get-tuple-element.73) | copy-start | bytes 147460
  18.5 9.0 %copy-start.21 = (f32[3,4096]{1,0:T(4,128)}, f32[3,4096]{1,0:T(4,128)S(1)}, u32[]{:S(2)}) copy-start(f32[3,4096]{1,0:T(4,128)S(1)} %get-tuple-element.74) | copy-start | bytes 147460
  18.5 9.0 %copy-start.23 = (f32[3,4096]{1,0:T(4,128)}, f32[3,4096]{1,0:T(4,128)S(1)}, u32[]{:S(2)}) copy-start(f32[3,4096]{1,0:T(4,128)S(1)} %get-tuple-element.75) | copy-start | bytes 147460
  18.6 8.9 %copy-start.25 = (f32[3,4096]{1,0:T(4,128)}, f32[3,4096]{1,0:T(4,128)S(1)}, u32[]{:S(2)}) copy-start(f32[3,4096]{1,0:T(4,128)S(1)} %get-tuple-element.76) | copy-start | bytes 147460
  18.6 8.9 %copy-start.27 = (f32[3,4096]{1,0:T(4,128)}, f32[3,4096]{1,0:T(4,128)S(1)}, u32[]{:S(2)}) copy-start(f32[3,4096]{1,0:T(4,128)S(1)} %get-tuple-element.77) | copy-start | bytes 147460
  22.1 31.4 %copy-start.12 = (bf16[3,128,4096]{1,2,0:T(8,128)(2,1)}, bf16[3,128,4096]{1,2,0:T(8,128)(2,1)S(1)}, u32[]{:S(2)}) copy-start(bf16[3,128,4096]{1,2,0:T(8,128)(2,1)S(1)} %copy.105) | copy-start | bytes 9437188
  53.6 1.7 copy-start.10
  56.8 52.0 %all-to-all-start = ((f32[16,256,128]{2,1,0:T(8,128)}), f32[16,256,128]{2,1,0:T(8,128)}, u32[]{:S(2)}, u32[]{:S(2)}) async-start(f32[16,256,128]{2,1,0:T(8,128)} %bitcast.237), calls=%async_computation | async-start | bytes 4194304 | tf_op jit(solution)/shard_map/all_to_all | solution.py:104
  159.8 14.5 %copy-start.9 = (f32[256,64,64]{0,2,1:T(8,128)}, f32[256,64,64]{0,2,1:T(8,128)S(1)}, u32[]{:S(2)}) copy-start(f32[256,64,64]{0,2,1:T(8,128)S(1)} %fusion.73) | copy-start | bytes 12582916
  218.3 52.3 %all-to-all-start.2 = ((f32[256,16,128]{0,2,1:T(8,128)}), f32[256,16,128]{0,2,1:T(8,128)}, u32[]{:S(2)}, u32[]{:S(2)}) async-start(f32[256,16,128]{0,2,1:T(8,128)} %bitcast.20), calls=%async_computation.2 | async-start | bytes 4194304 | tf_op jit(solution)/shard_map/all_to_all | solution.py:110
  229.6 43.9 %copy-start.11 = (bf16[3,128,4096]{1,2,0:T(8,128)(2,1)S(1)}, bf16[3,128,4096]{1,2,0:T(8,128)(2,1)}, u32[]{:S(2)}) copy-start(bf16[3,128,4096]{1,2,0:T(8,128)(2,1)} %copy-done.10) | copy-start | bytes 9437188
  232.0 48.6 %copy-start.30 = (f32[4096]{0:T(1024)S(1)}, f32[4096]{0:T(1024)}, u32[]{:S(2)}) copy-start(f32[4096]{0:T(1024)} %param.8) | copy-start | bytes 49156
  352.3 6.3 copy-start.15
  364.6 14.1 %copy-start.8 = (f32[256,64,64]{0,1,2:T(8,128)}, f32[256,64,64]{0,1,2:T(8,128)S(1)}, u32[]{:S(2)}) copy-start(f32[256,64,64]{0,1,2:T(8,128)S(1)} %get-tuple-element.45) | copy-start | bytes 12582916
  407.5 8.4 %copy-start.4 = (f32[256,64,64]{0,2,1:T(8,128)S(1)}, f32[256,64,64]{0,2,1:T(8,128)}, u32[]{:S(2)}) copy-start(f32[256,64,64]{0,2,1:T(8,128)} %get-tuple-element.32) | copy-start | bytes 12582916
  415.9 4.2 copy-start.7
  420.1 5.8 copy-start.5
  425.8 4.2 copy-start.6
  471.9 46.4 %all-to-all-start.4 = ((f32[256,16,128]{0,2,1:T(8,128)}), f32[256,16,128]{0,2,1:T(8,128)}, u32[]{:S(2)}, u32[]{:S(2)}) async-start(f32[256,16,128]{0,2,1:T(8,128)} %bitcast.238), calls=%async_computation.4 | async-start | bytes 4194304 | tf_op jit(solution)/shard_map/all_to_all | solution.py:133
  478.6 7.1 %copy-start.16 = (f32[256,64,64]{0,2,1:T(8,128)S(1)}, f32[256,64,64]{0,2,1:T(8,128)}, u32[]{:S(2)}) copy-start(f32[256,64,64]{0,2,1:T(8,128)} %get-tuple-element.41) | copy-start | bytes 12582916
  518.3 54.9 %all-to-all-start.5 = ((f32[256,16,128]{0,2,1:T(8,128)}), f32[256,16,128]{0,2,1:T(8,128)}, u32[]{:S(2)}, u32[]{:S(2)}) async-start(f32[256,16,128]{0,2,1:T(8,128)} %bitcast.236), calls=%async_computation.5 | async-start | bytes 4194304 | tf_op jit(solution)/shard_map/all_to_all | solution.py:134
  532.7 3.2 copy-start.13
  532.7 5.3 copy-start.14
  535.3 24.7 %copy-start = (f32[1,128,4096]{1,2,0:T(8,128)}, f32[1,128,4096]{1,2,0:T(8,128)S(1)}, u32[]{:S(2)}) copy-start(f32[1,128,4096]{1,2,0:T(8,128)S(1)} %get-tuple-element.58) | copy-start | bytes 6291460
  535.3 24.7 %copy-start.2 = (f32[1,128,4096]{1,2,0:T(8,128)}, f32[1,128,4096]{1,2,0:T(8,128)S(1)}, u32[]{:S(2)}) copy-start(f32[1,128,4096]{1,2,0:T(8,128)S(1)} %get-tuple-element.59) | copy-start | bytes 6291460
  571.9 73.8 %collective-permute-start.1 = (f32[3,6,4096]{2,1,0:T(8,128)S(1)}, f32[3,6,4096]{2,1,0:T(8,128)S(1)}, u32[]{:S(2)}, u32[]{:S(2)}) collective-permute-start(f32[3,6,4096]{2,1,0:T(8,128)S(1)} %copy.141), channel_id=1, source_target_pairs={{2,0},{4,2},{6,4},{8,6},{10,8},{12,10},{14,12},{16,14},{18,16},{20... | collective-permute-start | bytes 884744 | tf_op jit(solution)/shard_map/ppermute | solution.py:16
  649.6 10.7 %copy-start.1 = (f32[1,128,4096]{1,2,0:T(8,128)S(1)}, f32[1,128,4096]{1,2,0:T(8,128)}, u32[]{:S(2)}) copy-start(f32[1,128,4096]{1,2,0:T(8,128)} %copy-done) | copy-start | bytes 6291460
  649.6 10.7 %copy-start.3 = (f32[1,128,4096]{1,2,0:T(8,128)S(1)}, f32[1,128,4096]{1,2,0:T(8,128)}, u32[]{:S(2)}) copy-start(f32[1,128,4096]{1,2,0:T(8,128)} %copy-done.2) | copy-start | bytes 6291460
  649.6 10.7 %copy-start.18 = (f32[3,4096]{1,0:T(4,128)S(1)}, f32[3,4096]{1,0:T(4,128)}, u32[]{:S(2)}) copy-start(f32[3,4096]{1,0:T(4,128)} %copy-done.17) | copy-start | bytes 147460
  649.6 10.7 %copy-start.20 = (f32[3,4096]{1,0:T(4,128)S(1)}, f32[3,4096]{1,0:T(4,128)}, u32[]{:S(2)}) copy-start(f32[3,4096]{1,0:T(4,128)} %copy-done.19) | copy-start | bytes 147460
  649.7 10.7 %copy-start.22 = (f32[3,4096]{1,0:T(4,128)S(1)}, f32[3,4096]{1,0:T(4,128)}, u32[]{:S(2)}) copy-start(f32[3,4096]{1,0:T(4,128)} %copy-done.21) | copy-start | bytes 147460
  649.7 10.7 %copy-start.24 = (f32[3,4096]{1,0:T(4,128)S(1)}, f32[3,4096]{1,0:T(4,128)}, u32[]{:S(2)}) copy-start(f32[3,4096]{1,0:T(4,128)} %copy-done.23) | copy-start | bytes 147460
  649.7 10.7 %copy-start.26 = (f32[3,4096]{1,0:T(4,128)S(1)}, f32[3,4096]{1,0:T(4,128)}, u32[]{:S(2)}) copy-start(f32[3,4096]{1,0:T(4,128)} %copy-done.25) | copy-start | bytes 147460
  649.7 10.7 %copy-start.28 = (f32[3,4096]{1,0:T(4,128)S(1)}, f32[3,4096]{1,0:T(4,128)}, u32[]{:S(2)}) copy-start(f32[3,4096]{1,0:T(4,128)} %copy-done.27) | copy-start | bytes 147460
  649.7 10.7 %copy-start.29 = (f32[3,1,4096]{2,0,1:T(4,128)S(1)}, f32[3,1,4096]{2,0,1:T(4,128)}, u32[]{:S(2)}) copy-start(f32[3,1,4096]{2,0,1:T(4,128)} %copy.239) | copy-start | bytes 147460
where the time goes:
time: 699 us; the launch traced here: 693 us
  matrix products  245 us (35%)
  blocking collectives  134 us (19%)
  other arithmetic  105 us (15%)
  waiting for transfers between devices  90.7 us (13%)
  local copies, waits for them, and re-layouts  66.3 us (9%)
  starting transfers between devices  50.2 us (7%)
    dot_general x36, matrix products, contract(): return jnp.einsum(form, left, right, precision=lax.Precision.HIGHEST)  245 us
    psum x1, blocking collectives, on_device(): gain_grad, short_grads = lax.psum((gain_part, filt_part), 'ctx')  65.7 us
    all_to_all x1, blocking collectives, on_device(): lax.all_to_all(grad_conv.T, 'ctx', split_axis=0, concat_axis=1, tiled=True)  58.2 us
    all_to_all x1, waiting for transfers between devices, on_device(): lax.all_to_all(chan_z, 'ctx', split_axis=1, concat_axis=0, tiled=True)  38.6 us
    convert_element_type x1, other arithmetic, on_device(): grad_in.astype(jnp.bfloat16)  28.2 us
    all_to_all x1, waiting for transfers between devices, on_device(): lax.all_to_all(mixed_in.T, 'ctx', split_axis=0, concat_axis=1, tiled=True)  26.8 us
    convert_element_type x1, other arithmetic, on_device(): features = lax.optimization_barrier(conv_sum.astype(jnp.bfloat16))  26.1 us
    all_to_all x1, waiting for transfers between devices, on_device(): lax.all_to_all(chan_du, 'ctx', split_axis=1, concat_axis=0, tiled=True)  25.3 us
  transfers between devices with their start and end apart: 7, of which 3 were waited for; matrix products, arithmetic and copies ran while one was open for 17% of the time, Pallas kernels for 0%

commit v1 on v0

--- a/solution.py
+++ b/solution.py
@@ -1,3 +1,4 @@
+import functools
 import math
 import jax
 import jax.numpy as jnp
@@ -8,6 +9,17 @@
 GROUP = 16
 KS = 7
 epsilon = 1e-05
+
+
+def try_all_the_slot(block_here, at_axis, array_dim):
+    block_last = lax.all_to_all(
+        jnp.stack(jnp.split(block_here, lax.axis_size("ctx"), at_axis)), "ctx", 0, 0
+    )
+    left_arr = jnp.concatenate(block_last, axis=array_dim)
+    return left_arr
+
+
+series_map = functools.partial(try_all_the_slot, at_axis=0, array_dim=1)
 
 
 def passed_along(block, axis, distance):
@@ -101,7 +113,7 @@
     value_feat = features[2].astype(jnp.float32)
     mixed_in = key_feat * value_feat
     chan_h = lax.all_to_all(long_filter.T, "ctx", split_axis=0, concat_axis=1, tiled=True)
-    chan_u = lax.all_to_all(mixed_in.T, "ctx", split_axis=0, concat_axis=1, tiled=True)
+    chan_u = series_map(mixed_in.T)
     real_u, imag_u = forward_spectrum(chan_u, tables)
     real_h, imaginary_filter = forward_spectrum(chan_h, tables)
     prod_r = real_u * real_h - imag_u * imaginary_filter

time: 699 us -> 666 us (0.953)
  blocking collectives: 134 us -> 190 us
  other arithmetic: 105 us -> 51 us
  local copies, waits for them, and re-layouts: 66.3 us -> 37 us
  starting transfers between devices: 50.2 us -> 39.7 us
    all_to_all x0 -> x1, blocking collectives: none -> 58.4 us  [on_device(): lax.all_to_all(chan_z, 'ctx', split_axis=1, concat_axis=0, tiled=True)]
    all_to_all x2 -> x1, waiting for transfers between devices: 65.4 us -> 23.4 us  [try_all_the_slot(): lax.all_to_all(jnp.stack(jnp.split(block_here, lax.axis_size('ctx'), at_a...]
    all_to_all x1, waiting for transfers between devices: 0.01 us -> 24.5 us  [on_device(): lax.all_to_all(long_filter.T, 'ctx', split_axis=0, concat_axis=1, tiled=T...]
    all_to_all x1, waiting for transfers between devices: 0.01 us -> 20.9 us  [on_device(): lax.all_to_all(chan_dh, 'ctx', split_axis=1, concat_axis=0, tiled=True)]
    convert_element_type x1, other arithmetic: 26.1 us -> 7.1 us  [on_device(): features = lax.optimization_barrier(conv_sum.astype(jnp.bfloat16))]
    reduce_sum x1, other arithmetic: 21.9 us -> 8.49 us  [on_device(): tap_prod = jnp.sum(grad_feats * window, axis=1)]
    all_to_all x2 -> x1, starting transfers between devices: 22.3 us -> 11.7 us  [try_all_the_slot(): lax.all_to_all(jnp.stack(jnp.split(block_here, lax.axis_size('ctx'), at_a...]
    unnamed x81 -> x94, local copies, waits for them, and re-layouts: 24.7 us -> 14.2 us
  transfers between devices with their start and end apart: 7 -> 6, of which waited for: 3 -> 4; matrix products, arithmetic and copies ran while one was open for 17% -> 11% of each run, Pallas kernels for 0% -> 0%
where the time goes in v1:
time: 666 us; the launch traced here: 661 us
  matrix products  246 us (37%)
  blocking collectives  190 us (29%)
  waiting for transfers between devices  95.4 us (14%)
  other arithmetic  51 us (8%)
  starting transfers between devices  39.7 us (6%)
  local copies, waits for them, and re-layouts  37 us (6%)
    dot_general x36, matrix products, contract(): return jnp.einsum(form, left, right, precision=lax.Precision.HIGHEST)  246 us
    psum x1, blocking collectives, on_device(): gain_grad, short_grads = lax.psum((gain_part, filt_part), 'ctx')  69.2 us
    all_to_all x1, blocking collectives, on_device(): lax.all_to_all(chan_z, 'ctx', split_axis=1, concat_axis=0, tiled=True)  58.4 us
    all_to_all x1, blocking collectives, on_device(): lax.all_to_all(grad_conv.T, 'ctx', split_axis=0, concat_axis=1, tiled=True)  52.1 us
    all_to_all x1, waiting for transfers between devices, on_device(): lax.all_to_all(chan_du, 'ctx', split_axis=1, concat_axis=0, tiled=True)  26.7 us
    all_to_all x1, waiting for transfers between devices, on_device(): lax.all_to_all(long_filter.T, 'ctx', split_axis=0, concat_axis=1, tiled=T...  24.5 us
    all_to_all x1, waiting for transfers between devices, try_all_the_slot(): lax.all_to_all(jnp.stack(jnp.split(block_here, lax.axis_size('ctx'), at_a...  23.4 us
    all_to_all x1, waiting for transfers between devices, on_device(): lax.all_to_all(chan_dh, 'ctx', split_axis=1, concat_axis=0, tiled=True)  20.9 us
  transfers between devices with their start and end apart: 6, of which 4 were waited for; matrix products, arithmetic and copies ran while one was open for 11% of the time, Pallas kernels for 0%

profile of v1, /device:TPU:0, one launch (start us, length us, event | category | flops | bytes accessed | tf_op | source)
XLA Modules:
  0.0 660.6 jit_solution(4356061909955731773)
XLA Ops:
  8.4 6.6 all-to-all-start.1
  20.7 7.1 %fusion.6 = bf16[3,128,4096]{2,1,0:T(8,128)(2,1)S(1)} fusion(bf16[3,128,4096]{2,1,0:T(8,128)(2,1)S(1)} %copy-done.14, bf16[3,6,4096]{2,1,0:T(8,128)(2,1)} %collective-permute-done, f32[3,4096]{1,0:T(4,128)S(1)} %get-tuple-element.67, f32[3,4096]{1,0:T(4,128)S(1)} %get-tuple-element.68, f32[3,4096]{1,0:T(4,128)S(1)} %get-tuple-element.69, ...), kind=kLoop, calls=%fused_computation.26 | loop fusion | flops 61341696 | bytes 6782976 | tf_op jit(solution)/shard_map/convert_element_type | solution.py:110
  31.5 24.5 %all-to-all-done.1 = f32[16,256,128]{2,1,0:T(8,128)} async-done(((f32[16,256,128]{2,1,0:T(8,128)}), f32[16,256,128]{2,1,0:T(8,128)}, u32[]{:S(2)}, u32[]{:S(2)}) %all-to-all-start.1) | async-done | bytes 2097184 | tf_op jit(solution)/shard_map/all_to_all | solution.py:115
  56.0 11.7 %all-to-all-start = ((f32[16,256,128]{1,2,0:T(8,128)}), f32[16,256,128]{1,2,0:T(8,128)S(1)}, u32[]{:S(2)}, u32[]{:S(2)}) async-start(f32[16,256,128]{1,2,0:T(8,128)} %copy-done.16), calls=%async_computation | async-start | bytes 4194304 | tf_op jit(solution)/shard_map/all_to_all | solution.py:15
  71.2 8.3 %fusion.93 = f32[64,256,64]{1,0,2:T(8,128)} fusion(f32[256,32,64]{0,2,1:T(8,128)} %bitcast.298, f32[64,64]{0,1:T(8,128)S(1)} %fusion.166), kind=kOutput, calls=%fused_computation.147 | convolution fusion | flops 402653184 | bytes 6307840 | tf_op jit(solution)/shard_map/cnb,kn->ckb/dot_general | solution.py:32
  79.5 5.8 fusion.95
  85.3 23.4 %all-to-all-done = f32[16,256,128]{1,2,0:T(8,128)S(1)} async-done(((f32[16,256,128]{1,2,0:T(8,128)}), f32[16,256,128]{1,2,0:T(8,128)S(1)}, u32[]{:S(2)}, u32[]{:S(2)}) %all-to-all-start) | async-done | bytes 2097184 | tf_op jit(solution)/shard_map/all_to_all | solution.py:15
  108.7 5.8 fusion.97
  114.5 9.0 %add_bitcast_fusion.1 = (f32[256,64,64]{0,1,2:T(8,128)S(1)}, f32[256,64,64]{0,1,2:T(8,128)S(1)}, f32[256,64,64]{0,1,2:T(8,128)S(1)}, f32[256,64,64]{0,1,2:T(8,128)S(1)}) fusion(f32[64,256,64]{1,0,2:T(8,128)} %fusion.95, f32[64,256,64]{1,0,2:T(8,128)} %fusion.93, f32[64,64]{0,1:T(8,128)S(1)} %get-tuple-element.73, f32[64,64]{0,1:T(8,128)S(1)} %get-tuple-element.74, ...), kind=kOutput, calls=%fused_computation.75 | convolution fusion | flops 417333248 | bytes 31539200 | tf_op jit(solution)/shard_map/cnb,kn->ckb/dot_general | solution.py:32
  123.5 6.4 fusion.41
  129.9 6.9 %fusion.43 = f32[256,64,64]{0,2,1:T(8,128)S(1)} fusion(f32[256,64,64]{0,1,2:T(8,128)S(1)} %get-tuple-element.45), kind=kOutput, calls=%fused_computation.88 | convolution fusion | flops 805363712 | bytes 8388608 | tf_op jit(solution)/shard_map/ckb,bm->ckm/dot_general | solution.py:32
  136.8 7.2 %fusion.49 = f32[256,64,64]{0,2,1:T(8,128)} fusion(f32[256,64,64]{0,1,2:T(8,128)S(1)} %get-tuple-element.64), kind=kOutput, calls=%fused_computation.94 | convolution fusion | flops 805363712 | bytes 8388608 | tf_op jit(solution)/shard_map/ckb,bm->ckm/dot_general | solution.py:32
  144.0 6.5 fusion.51
  150.5 7.3 %fusion.73 = f32[256,64,64]{0,2,1:T(8,128)S(1)} fusion(f32[256,64,64]{0,2,1:T(8,128)S(1)} %fusion.41, f32[256,64,64]{0,1,2:T(8,128)S(1)} %get-tuple-element.44), kind=kOutput, calls=%fused_computation.120 | convolution fusion | flops 806412288 | bytes 12582912 | tf_op jit(solution)/shard_map/ckb,bm->ckm/dot_general | solution.py:32
  157.8 7.2 %fusion.70 = f32[256,64,64]{0,2,1:T(8,128)} fusion(f32[256,64,64]{0,2,1:T(8,128)S(1)} %fusion.43, f32[256,64,64]{0,1,2:T(8,128)S(1)} %get-tuple-element.44), kind=kOutput, calls=%fused_computation.119 | convolution fusion | flops 806412288 | bytes 12582912 | tf_op jit(solution)/shard_map/ckb,bm->ckm/dot_general | solution.py:32
  165.0 7.2 %fusion.64 = f32[256,64,64]{0,2,1:T(8,128)} fusion(f32[256,64,64]{0,2,1:T(8,128)S(1)} %fusion.51, f32[256,64,64]{0,1,2:T(8,128)S(1)} %get-tuple-element.65), kind=kOutput, calls=%fused_computation.117 | convolution fusion | flops 806412288 | bytes 12582912 | tf_op jit(solution)/shard_map/ckb,bm->ckm/dot_general | solution.py:32
  172.3 11.9 %multiply_add_fusion.5 = (f32[256,64,64]{0,2,1:T(8,128)S(1)}, f32[256,64,64]{0,2,1:T(8,128)S(1)}, f32[256,64,64]{0,2,1:T(8,128)}) fusion(f32[256,64,64]{0,2,1:T(8,128)} %fusion.70, f32[256,64,64]{0,2,1:T(8,128)} %fusion.64, f32[256,64,64]{0,2,1:T(8,128)S(1)} %fusion.73, f32[256,64,64]{0,2,1:T(8,128)} %fusion.49, f32[256,64,64]{0,1,2:T(8,128)S(1)} %get-tuple-element.65), kind=kOutput, calls=%fused_computation.72 | convolution fusion | flops 812703744 | bytes 33554432 | tf_op jit(solution)/shard_map/ckb,bm->ckm/dot_general | solution.py:32
  193.0 4.8 convolution_subtract_fusion.2
  197.8 6.6 multiply_subtract_fusion.4
  204.3 4.5 fusion.29
  208.9 4.9 multiply_bitcast_fusion.2
  215.0 58.4 %all_to_all.94 = f32[256,16,128]{0,2,1:T(8,128)S(1)} all-to-all(f32[256,16,128]{0,2,1:T(8,128)S(1)} %bitcast.305), channel_id=1, replica_groups=mesh['ctx'=16,'ch'=2] {'ctx'}, dimensions={1} | all-to-all | bytes 4194304 | tf_op jit(solution)/shard_map/all_to_all | solution.py:122
  275.4 5.0 psum.28
  283.1 4.9 psum.29
  292.4 52.1 %all_to_all.95 = f32[16,256,128]{1,2,0:T(8,128)S(1)} all-to-all(f32[16,256,128]{1,2,0:T(8,128)S(1)} %bitcast.307), channel_id=1, replica_groups=mesh['ctx'=16,'ch'=2] {'ctx'}, dimensions={0} | all-to-all | bytes 4194304 | tf_op jit(solution)/shard_map/all_to_all | solution.py:135
  344.4 4.6 fusion.89
  349.0 6.0 add_bitcast_fusion
  355.0 6.9 %fusion.33 = f32[256,64,64]{0,2,1:T(8,128)S(1)} fusion(f32[256,64,64]{0,1,2:T(8,128)S(1)} %get-tuple-element.41), kind=kOutput, calls=%fused_computation.78 | convolution fusion | flops 805363712 | bytes 8388608 | tf_op jit(solution)/shard_map/ckb,bm->ckm/dot_general | solution.py:32
  361.9 7.2 %fusion.35 = f32[256,64,64]{0,2,1:T(8,128)} fusion(f32[256,64,64]{0,1,2:T(8,128)S(1)} %get-tuple-element.41), kind=kOutput, calls=%fused_computation.80 | convolution fusion | flops 805363712 | bytes 8388608 | tf_op jit(solution)/shard_map/ckb,bm->ckm/dot_general | solution.py:32
  369.1 7.3 %fusion.79 = f32[256,64,64]{0,2,1:T(8,128)} fusion(f32[256,64,64]{0,2,1:T(8,128)S(1)} %fusion.33, f32[256,64,64]{0,1,2:T(8,128)S(1)} %get-tuple-element.40), kind=kOutput, calls=%fused_computation.122 | convolution fusion | flops 806412288 | bytes 12582912 | tf_op jit(solution)/shard_map/ckb,bm->ckm/dot_general | solution.py:32
  376.4 21.4 %multiply_subtract_fusion.1 = (f32[256,64,64]{0,2,1:T(8,128)}, f32[256,64,64]{0,2,1:T(8,128)}, f32[256,64,64]{0,2,1:T(8,128)}, f32[256,64,64]{0,2,1:T(8,128)}) fusion(f32[256,64,64]{0,2,1:T(8,128)} %get-tuple-element.66, f32[256,64,64]{0,2,1:T(8,128)} %fusion.64, f32[256,64,64]{0,2,1:T(8,128)} %fusion.79, f32[256,64,64]{0,2,1:T(8,128)} %copy-done.7, ...), kind=kOutput, calls=%fused_computation.62 | convolution fusion | flops 818995200 | bytes 46137344 | tf_op jit(solution)/shard_map/ckb,bm->ckm/dot_general | solution.py:32
  397.8 8.4 %fusion.139 = f32[256,64,64]{0,2,1:T(8,128)} fusion(f32[256,64,64]{0,2,1:T(8,128)} %get-tuple-element.26), kind=kOutput, calls=%fused_computation.225 | convolution fusion | flops 805363712 | bytes 8388608 | tf_op jit(solution)/shard_map/ckb,bm->ckm/dot_general | solution.py:32
  410.4 5.8 convolution_subtract_fusion
  424.6 5.6 convolution_subtract_fusion.1
  430.2 5.8 convolution_add_fusion.1
  436.0 11.6 %multiply_subtract_fusion = (f32[256,64,64]{0,2,1:T(8,128)}, f32[256,64,64]{0,2,1:T(8,128)}, f32[256,64,64]{0,2,1:T(8,128)}, f32[256,64,64]{0,2,1:T(8,128)S(1)}) fusion(f32[256,64,64]{0,2,1:T(8,128)} %convolution_subtract_fusion, f32[64,64]{1,0:T(8,128)S(1)} %copy.79, f32[64,64]{1,0:T(8,128)S(1)} %copy.78, f32[256,64,64]{0,2,1:T(8,128)} %convolution_subtract_fusion.1, ...), kind=kOutput, calls=%fused_computation.61 | convolution fusion | flops 818995200 | bytes 37781504 | tf_op jit(solution)/shard_map/ckb,bm->ckm/dot_general | solution.py:32
  447.6 7.4 %fusion.25 = f32[32,256,64]{1,0,2:T(8,128)S(1)} fusion(f32[256,64,64]{0,2,1:T(8,128)} %get-tuple-element.62, f32[64,64]{0,1:T(8,128)S(1)} %fusion.166), kind=kOutput, calls=%fused_computation.52 | convolution fusion | flops 402653184 | bytes 6307840 | tf_op jit(solution)/shard_map/ckb,kn->cnb/dot_general | solution.py:32
  455.0 4.7 multiply_bitcast_fusion.1
  462.3 5.4 all-to-all-start.4
  467.7 7.1 %fusion.21 = f32[32,256,64]{1,0,2:T(8,128)S(1)} fusion(f32[256,64,64]{0,2,1:T(8,128)} %get-tuple-element.37, f32[64,64]{0,1:T(8,128)S(1)} %fusion.166), kind=kOutput, calls=%fused_computation.48 | convolution fusion | flops 402653184 | bytes 6307840 | tf_op jit(solution)/shard_map/ckb,kn->cnb/dot_general | solution.py:32
  474.8 4.7 multiply_bitcast_fusion
  482.0 26.7 %all-to-all-done.4 = f32[256,16,128]{0,2,1:T(8,128)} async-done(((f32[256,16,128]{0,2,1:T(8,128)}), f32[256,16,128]{0,2,1:T(8,128)}, u32[]{:S(2)}, u32[]{:S(2)}) %all-to-all-start.4) | async-done | bytes 2097184 | tf_op jit(solution)/shard_map/all_to_all | solution.py:145
  508.7 11.5 %all-to-all-start.5 = ((f32[256,16,128]{0,2,1:T(8,128)}), f32[256,16,128]{0,2,1:T(8,128)}, u32[]{:S(2)}, u32[]{:S(2)}) async-start(f32[256,16,128]{0,2,1:T(8,128)} %bitcast.303), calls=%async_computation.5 | async-start | bytes 4194304 | tf_op jit(solution)/shard_map/all_to_all | solution.py:146
  525.6 8.5 %fusion.12 = (f32[3,4096]{1,0:T(4,128)S(1)}, f32[3,4096]{1,0:T(4,128)S(1)}, f32[3,4096]{1,0:T(4,128)S(1)}, f32[3,4096]{1,0:T(4,128)S(1)}, f32[3,4096]{1,0:T(4,12...) fusion(bf16[3,128,4096]{2,1,0:T(8,128)(2,1)S(1)} %copy-done.15, bf16[3,6,4096]{2,1,0:T(8,128)(2,1)} %collective-permute-done, ...), kind=kLoop, calls=%fused_computation.32 | loop fusion | flops 64401408 | bytes 9928704 | tf_op jit(solution)/shard_map/reduce_sum | solution.py:161
  540.3 20.9 %all-to-all-done.5 = f32[256,16,128]{0,2,1:T(8,128)} async-done(((f32[256,16,128]{0,2,1:T(8,128)}), f32[256,16,128]{0,2,1:T(8,128)}, u32[]{:S(2)}, u32[]{:S(2)}) %all-to-all-start.5) | async-done | bytes 2097184 | tf_op jit(solution)/shard_map/all_to_all | solution.py:146
  567.3 69.2 %all-reduce = (f32[3,7,256]{2,0,1:T(4,128)S(1)}, f32[4096]{0:T(1024)}) all-reduce(f32[3,7,256]{2,0,1:T(4,128)S(1)} %constant_dynamic-update-slice_fusion, f32[4096]{0:T(1024)S(1)} %get-tuple-element.22), channel_id=1, replica_groups=mesh['ctx'=16,'ch'=2] {'ctx'}, use_global_device_ids=true, to_apply=%region_18.19 | all-reduce | flops 9472 | bytes 75776 | tf_op jit(solution)/shard_map/psum | solution.py:164
  637.2 4.7 pad_maximum_fusion
  641.9 18.4 %fusion.15 = bf16[3,128,4096]{2,1,0:T(8,128)(2,1)} fusion(f32[3,134,4096]{2,1,0:T(8,128)} %pad_maximum_fusion, f32[3,4096]{1,0:T(4,128)S(1)} %copy-done.18, f32[3,4096]{1,0:T(4,128)S(1)} %copy-done.20, f32[3,4096]{1,0:T(4,128)S(1)} %copy-done.22, f32[3,4096]{1,0:T(4,128)S(1)} %copy-done.24, f32[3,4096]{1,0:T(4,128)S(1)} %copy-done.26, ...), kind=kLoop, calls=%fused_computation.36 | loop fusion | flops 25165824 | bytes 47529984 | tf_op jit(solution)/shard_map/convert_element_type | solution.py:165
  (145 shorter events, 75.3 us)
Async XLA Ops:
  2.3 12.7 %copy-start.32 = (f32[3,7,256]{2,1,0:T(8,128)S(1)}, f32[3,7,256]{2,1,0:T(8,128)}, u32[]{:S(2)}) copy-start(f32[3,7,256]{2,1,0:T(8,128)} %param.6) | copy-start | bytes 64516
  2.3 18.4 %collective-permute-start = (bf16[3,6,4096]{2,1,0:T(8,128)(2,1)}, bf16[3,6,4096]{2,1,0:T(8,128)(2,1)}, u32[]{:S(2)}, u32[]{:S(2)}) collective-permute-start(bf16[3,6,4096]{2,1,0:T(8,128)(2,1)} %slice.123), channel_id=1, source_target_pairs={{0,2},{2,4},{4,6},{6,8},{8,10},{10,12},{12,14},{14,16},{16,18},{18... | collective-permute-start | bytes 442376 | tf_op jit(solution)/shard_map/ppermute | solution.py:28
  8.4 47.6 %all-to-all-start.1 = ((f32[16,256,128]{2,1,0:T(8,128)}), f32[16,256,128]{2,1,0:T(8,128)}, u32[]{:S(2)}, u32[]{:S(2)}) async-start(f32[16,256,128]{2,1,0:T(8,128)} %bitcast.30), calls=%async_computation.1 | async-start | bytes 4194304 | tf_op jit(solution)/shard_map/all_to_all | solution.py:115
  15.0 5.8 copy-start.14
  20.4 9.3 %copy-start.17 = (f32[3,4096]{1,0:T(4,128)}, f32[3,4096]{1,0:T(4,128)S(1)}, u32[]{:S(2)}) copy-start(f32[3,4096]{1,0:T(4,128)S(1)} %get-tuple-element.67) | copy-start | bytes 147460
  20.5 9.3 %copy-start.19 = (f32[3,4096]{1,0:T(4,128)}, f32[3,4096]{1,0:T(4,128)S(1)}, u32[]{:S(2)}) copy-start(f32[3,4096]{1,0:T(4,128)S(1)} %get-tuple-element.68) | copy-start | bytes 147460
  20.5 9.2 %copy-start.21 = (f32[3,4096]{1,0:T(4,128)}, f32[3,4096]{1,0:T(4,128)S(1)}, u32[]{:S(2)}) copy-start(f32[3,4096]{1,0:T(4,128)S(1)} %get-tuple-element.69) | copy-start | bytes 147460
  20.5 9.2 %copy-start.23 = (f32[3,4096]{1,0:T(4,128)}, f32[3,4096]{1,0:T(4,128)S(1)}, u32[]{:S(2)}) copy-start(f32[3,4096]{1,0:T(4,128)S(1)} %get-tuple-element.70) | copy-start | bytes 147460
  20.6 9.2 %copy-start.25 = (f32[3,4096]{1,0:T(4,128)}, f32[3,4096]{1,0:T(4,128)S(1)}, u32[]{:S(2)}) copy-start(f32[3,4096]{1,0:T(4,128)S(1)} %get-tuple-element.71) | copy-start | bytes 147460
  20.6 9.2 %copy-start.27 = (f32[3,4096]{1,0:T(4,128)}, f32[3,4096]{1,0:T(4,128)S(1)}, u32[]{:S(2)}) copy-start(f32[3,4096]{1,0:T(4,128)S(1)} %get-tuple-element.72) | copy-start | bytes 147460
  20.7 9.1 %copy-start.29 = (f32[3,1,4096]{2,0,1:T(4,128)}, f32[3,1,4096]{2,0,1:T(4,128)S(1)}, u32[]{:S(2)}) copy-start(f32[3,1,4096]{2,0,1:T(4,128)S(1)} %copy.194) | copy-start | bytes 147460
  27.8 1.7 copy-start.8
  30.1 1.4 copy-start.16
  56.0 52.7 %all-to-all-start = ((f32[16,256,128]{1,2,0:T(8,128)}), f32[16,256,128]{1,2,0:T(8,128)S(1)}, u32[]{:S(2)}, u32[]{:S(2)}) async-start(f32[16,256,128]{1,2,0:T(8,128)} %copy-done.16), calls=%async_computation | async-start | bytes 4194304 | tf_op jit(solution)/shard_map/all_to_all | solution.py:15
  71.2 8.3 %copy-start.12 = (f32[256,16,128]{0,2,1:T(8,128)S(1)}, f32[256,16,128]{0,2,1:T(8,128)}, u32[]{:S(2)}) copy-start(f32[256,16,128]{0,2,1:T(8,128)} %copy.69) | copy-start | bytes 6291460
  157.8 14.5 %copy-start.7 = (f32[256,64,64]{0,2,1:T(8,128)}, f32[256,64,64]{0,2,1:T(8,128)S(1)}, u32[]{:S(2)}) copy-start(f32[256,64,64]{0,2,1:T(8,128)S(1)} %fusion.73) | copy-start | bytes 12582916
  215.0 60.0 %copy-start.9 = (bf16[3,128,4096]{2,1,0:T(8,128)(2,1)S(1)}, bf16[3,128,4096]{2,1,0:T(8,128)(2,1)}, u32[]{:S(2)}) copy-start(bf16[3,128,4096]{2,1,0:T(8,128)(2,1)} %copy-done.8) | copy-start | bytes 9437188
  273.4 7.0 %copy-start.31 = (f32[4096]{0:T(1024)S(1)}, f32[4096]{0:T(1024)}, u32[]{:S(2)}) copy-start(f32[4096]{0:T(1024)} %param.8) | copy-start | bytes 49156
  273.6 1.3 copy-start.11
  355.0 14.1 %copy-start.6 = (f32[256,64,64]{0,1,2:T(8,128)}, f32[256,64,64]{0,1,2:T(8,128)S(1)}, u32[]{:S(2)}) copy-start(f32[256,64,64]{0,1,2:T(8,128)S(1)} %get-tuple-element.40) | copy-start | bytes 12582916
  397.8 8.4 %copy-start.2 = (f32[256,64,64]{0,2,1:T(8,128)S(1)}, f32[256,64,64]{0,2,1:T(8,128)}, u32[]{:S(2)}) copy-start(f32[256,64,64]{0,2,1:T(8,128)} %get-tuple-element.27) | copy-start | bytes 12582916
  406.2 4.2 copy-start.5
  410.4 5.8 copy-start.3
  416.2 4.2 copy-start.4
  462.3 46.4 %all-to-all-start.4 = ((f32[256,16,128]{0,2,1:T(8,128)}), f32[256,16,128]{0,2,1:T(8,128)}, u32[]{:S(2)}, u32[]{:S(2)}) async-start(f32[256,16,128]{0,2,1:T(8,128)} %bitcast.304), calls=%async_computation.4 | async-start | bytes 4194304 | tf_op jit(solution)/shard_map/all_to_all | solution.py:145
  467.7 7.1 %copy-start.13 = (f32[256,64,64]{0,2,1:T(8,128)S(1)}, f32[256,64,64]{0,2,1:T(8,128)}, u32[]{:S(2)}) copy-start(f32[256,64,64]{0,2,1:T(8,128)} %get-tuple-element.36) | copy-start | bytes 12582916
  508.7 52.5 %all-to-all-start.5 = ((f32[256,16,128]{0,2,1:T(8,128)}), f32[256,16,128]{0,2,1:T(8,128)}, u32[]{:S(2)}, u32[]{:S(2)}) async-start(f32[256,16,128]{0,2,1:T(8,128)} %bitcast.303), calls=%async_computation.5 | async-start | bytes 4194304 | tf_op jit(solution)/shard_map/all_to_all | solution.py:146
  520.1 2.5 copy-start.10
  522.7 2.9 copy-start.15
  523.2 10.9 %copy-start = (f32[1,128,4096]{2,1,0:T(8,128)}, f32[1,128,4096]{2,1,0:T(8,128)S(1)}, u32[]{:S(2)}) copy-start(f32[1,128,4096]{2,1,0:T(8,128)S(1)} %get-tuple-element.53) | copy-start | bytes 6291460
  523.2 10.9 %copy-start.1 = (f32[1,128,4096]{2,1,0:T(8,128)}, f32[1,128,4096]{2,1,0:T(8,128)S(1)}, u32[]{:S(2)}) copy-start(f32[1,128,4096]{2,1,0:T(8,128)S(1)} %get-tuple-element.54) | copy-start | bytes 6291460
  538.9 98.3 %collective-permute-start.1 = (f32[3,6,4096]{2,1,0:T(8,128)S(1)}, f32[3,6,4096]{2,1,0:T(8,128)S(1)}, u32[]{:S(2)}, u32[]{:S(2)}) collective-permute-start(f32[3,6,4096]{2,1,0:T(8,128)S(1)} %slice.169), channel_id=1, source_target_pairs={{2,0},{4,2},{6,4},{8,6},{10,8},{12,10},{14,12},{16,14},{18,16},{20... | collective-permute-start | bytes 884744 | tf_op jit(solution)/shard_map/ppermute | solution.py:28
  637.2 4.7 copy-start.18
  637.2 4.7 copy-start.20
  637.2 4.7 copy-start.22
  637.2 4.7 copy-start.24
  637.2 4.7 copy-start.26
  637.2 4.7 copy-start.28
  637.2 4.7 copy-start.30
